TPU v7x, 128 devices: a whole 4x4x4 slice. The times are simulated.
128 devices in a mesh: row: 8 (over x, core), col: 16 (over y, z).
Axes of the slice: x: 4, y: 4, z: 4, core: 2. Of those that a mesh axis runs over, the one named last changes fastest.
Arguments:
- hamiltonian: float32 [16384, 2048], P('row', 'col'), may hold values from -0.09375 to 0.09375
- pattern: int32 [512, 64], P('row', 'col'), may hold values 0 or 1
- onsite: float32 [16384], P('row'), may hold values from -1 to 1
- members: int32 [128, 32], replicated, may hold values from 0 to 63, as said below
- orders: int32 [128], replicated, may hold values from 16 to 32, as said below
- intersection_inv: bfloat16 [16384, 3, 2048], P(('row', 'col')), may hold values from -6 to 6
Outputs:
- density: float32 [16384, 3, 2048], P(('row', 'col'))
Inputs may be any that keep to these rules, and one draw needn't show every extreme that they name: `members`: each row holds 32 distinct team block indices; the first 4 of row g are (g mod 16) * 4 onward in rising order. `orders`: some group has all 32 members active.
All inputs are finite; a program needn't handle non-finite values. No bound on the sum of `pattern` on one device may be relied on, other than what follows from the above.
Results may differ from a plain program's by a relative error of at most 0.0027.
Values may be sent and summed in bfloat16 or wider, within the bound.
A program may use at most 256 MiB of HBM per device.

v0:
```python
import jax
import jax.numpy as jnp
from jax import lax
from jax.experimental import pallas as pl
from jax.experimental.pallas import tpu as pltpu
from jax.sharding import PartitionSpec as P

BLOCK = 32
OWN_BLOCKS = 4
MEMBERS = 32
SLOTS = 16
TEAMS = 8
TEAM_BLOCKS = 64
TEAM_WIDTH = 2048
SUB = MEMBERS * BLOCK
OWN = OWN_BLOCKS * BLOCK
TILES = SUB // OWN
F32 = jnp.float32
BF16 = jnp.bfloat16
MESH = pl.DeviceIdType.MESH
SHARED = 12
LEAD = 10
RING_K = ((0, 3), (0, 1), (3, 2), (1, 2))


class Gather:
    def __init__(self, region, rows, send_sems, recv_sems, device):
        self.region, self.rows, self.device = region, rows, device
        self.send_sems, self.recv_sems = send_sems, recv_sems
        self.got = {(0, 0): {0, 1}}

    def copy(self, half, ring, k):
        source, landing = RING_K[k]
        step = 1 if k in (0, 2) else -1
        rows = self.rows // 2
        start, size = half * rows, rows
        if k >= 2:
            size = rows // 2
            start += size * (k - 2)

        def spot(offset):
            a, b = (offset, 0) if ring == 0 else (ring - 1, offset)
            return (b, a) if half == 0 else (a, b)

        along_z = (half == 0) == (ring == 0)
        n = half * 20 + ring * 4 + k
        return pltpu.make_async_remote_copy(
            src_ref=self.region(*spot(source), start, size),
            dst_ref=self.region(*spot(landing), start, size),
            send_sem=self.send_sems.at[n],
            recv_sem=self.recv_sems.at[n],
            device_id=self.device(0, step) if along_z else self.device(step, 0),
            device_id_type=MESH,
        ), spot(landing)

    def begin(self):
        for ring in (0, 1):
            for half in (0, 1):
                for k in (0, 1):
                    self.copy(half, ring, k)[0].start()

    def steps(self):
        order = [(0, 0), (0, 1), (1, 0), (1, 1), (0, 2), (0, 3), (4, 0), (4, 1), (2, 0), (2, 1), (1, 2), (1, 3)]
        order += [(3, 0), (3, 1), (4, 2), (4, 3), (2, 2), (2, 3), (3, 2), (3, 3)]
        seen = {}
        for ring, k in order:
            for half in (0, 1):
                copy, spot = self.copy(half, ring, k)
                copy.wait_recv()
                if k < 2:
                    self.copy(half, ring, k + 2)[0].start()
                whole = k < 2 or (half, ring, 5 - k) in seen
                seen[half, ring, k] = True
                done = None
                if ring == 0 and whole:
                    for j in (0, 1):
                        self.copy(half, RING_K[k][1] + 1, j)[0].start()
                if whole:
                    halves = self.got.setdefault(spot, set())
                    halves.add(half)
                    done = spot if len(halves) == 2 else None
                yield done

    def finish(self):
        for half in (0, 1):
            for ring in range(5):
                for k in range(4):
                    self.copy(half, ring, k)[0].wait_send()


def places():
    row, col = lax.axis_index("row"), lax.axis_index("col")
    y, z = col // 4, col % 4

    def device(dy, dz):
        return (row, ((y + dy + 4) % 4) * 4 + (z + dz + 4) % 4)

    return row, col, y, z, device


def greet(devices):
    barrier = pltpu.get_barrier_semaphore()
    for device in devices:
        pl.semaphore_signal(barrier, inc=1, device_id=device, device_id_type=MESH)
    pl.semaphore_wait(barrier, len(devices))


def sign_kernel(
    table, active, ham, pattern, onsite, out, own, onsites, left, rolled, turned, mat, diag, send_sems, recv_sems, *bufs
):
    row, col, y, z, device = places()
    near = [device(1, 0), device(3, 0), device(0, 1), device(0, 3)]
    lanes = lax.broadcasted_iota(jnp.int32, (OWN_BLOCKS, OWN), 1) // BLOCK
    spread = (lanes == lax.broadcasted_iota(jnp.int32, (OWN_BLOCKS, OWN), 0)).astype(F32)
    weights = lax.dot_general(
        pattern[...].astype(F32), spread, (((0,), (0,)), ((), ())), preferred_element_type=F32
    )
    for a in range(TEAM_BLOCKS):
        masked = ham[a * BLOCK : (a + 1) * BLOCK, :] * weights[a : a + 1, :]
        own[a] = masked
        bufs[0][a] = masked.astype(BF16)
    greet(near)
    gather = Gather(
        lambda oy, oz, start, size: bufs[oy * 4 + oz].at[pl.ds(start, size)], TEAM_BLOCKS, send_sems, recv_sems, device
    )
    gather.begin()
    for s in range(4):
        onsites[s * SLOTS : (s + 1) * SLOTS] = pltpu.roll(onsite[...], s * BLOCK, axis=1).reshape(SLOTS, 1, OWN)
    one_row = lax.broadcasted_iota(jnp.int32, (1, OWN), 1) // BLOCK

    def blocks(read, tile):
        pieces = [read(table[0, tile * 4 + q]).astype(F32) * active[0, tile * 4 + q] for q in range(4)]
        return jnp.concatenate(pieces, axis=0)

    @pl.loop(0, TILES)
    def _(tile):
        at = pl.ds(pl.multiple_of(tile * OWN, OWN), OWN)
        left[:, at] = blocks(lambda m: own[m], tile).T
        picked = jnp.zeros((1, OWN), F32)
        for q in range(4):
            line = onsites[table[3, tile * 4 + q]] * active[0, tile * 4 + q]
            picked = jnp.where(one_row == q, line, picked)
        diag[:, at] = picked

    def take_in(oy, oz):
        slot = oy * 4 + oz

        @pl.loop(0, TILES)
        def _(tile):
            x = blocks(lambda m: bufs[slot][m], tile)
            turned[slot, tile] = x.T.astype(BF16).reshape(4, BLOCK, OWN)
            rolled[slot * 4, tile] = x.astype(BF16)
            for s in (1, 2, 3):
                rolled[slot * 4 + s, tile] = pltpu.roll(x, s * BLOCK, axis=1).astype(BF16)

    take_in(0, 0)
    for spot in gather.steps():
        if spot:
            take_in(*spot)
    gather.finish()

    which = lax.broadcasted_iota(jnp.int32, (OWN, OWN), 1) // BLOCK
    eye = lax.broadcasted_iota(jnp.int32, (OWN, OWN), 0) == lax.broadcasted_iota(jnp.int32, (OWN, OWN), 1)

    def direct(up, across):
        tile = None
        for q in range(4):
            piece = rolled[table[1, across * 4 + q], up].astype(F32) * active[0, across * 4 + q]
            tile = piece if tile is None else jnp.where(which == q, piece, tile)
        return tile

    def mirrored(up, across):
        pieces = []
        for q in range(4):
            a = up * 4 + q
            pieces.append(turned[table[2, a], across, table[4, a]].astype(F32) * active[0, a])
        return jnp.concatenate(pieces, axis=0)

    def assemble(n, total):
        up, across = n // TILES, n % TILES
        tile = 0.5 * (direct(up, across) + mirrored(up, across))
        mat[pl.ds(pl.multiple_of(up * OWN, OWN), OWN), pl.ds(pl.multiple_of(across * OWN, OWN), OWN)] = tile.astype(
            BF16
        )
        return total + jnp.sum((tile * tile).reshape(OWN // 8, 8, OWN), axis=0)

    total = lax.fori_loop(0, TILES * TILES, assemble, jnp.zeros((8, OWN), F32))

    extra = jnp.zeros((1, OWN), F32)
    start = []
    for tile in range(TILES):
        at = slice(tile * OWN, (tile + 1) * OWN)
        on_diag = jnp.sum(jnp.where(eye, mat[at, at].astype(F32), 0.0), axis=0, keepdims=True)
        energy = diag[:, at]
        extra += energy * (2.0 * on_diag + energy)
        first = 0.5 * (left[:, at] + direct(0, tile))
        if tile == 0:
            first += jnp.where(eye, energy, 0.0)
        start.append(first)
    squares = jnp.sum(jnp.sum(total, axis=0, keepdims=True) + extra, axis=1, keepdims=True)
    scale = jnp.sqrt(active[1, 0] / (4.0 * (squares + 1e-06)))
    energy = diag[...]

    def apply(x):
        high = x.astype(BF16)
        low = (x - high.astype(F32)).astype(BF16)
        y = jnp.dot(jnp.concatenate([high, low], axis=0), mat[...], preferred_element_type=F32)
        return scale * (y[:OWN] + y[OWN:] + x * energy)

    initial = scale * jnp.concatenate(start, axis=1)
    first_step = 1.5 * initial - 0.5 * apply(apply(initial))
    once = apply(first_step)
    once = 1.5 * once - 0.5 * apply(apply(once))
    twice = apply(once)
    twice = 1.5 * twice - 0.5 * apply(apply(twice))
    result = 1.5 * first_step - 0.5 * twice
    for tile in range(TILES):
        at = slice(tile * OWN, (tile + 1) * OWN)
        out[at, :] = result[:, at].T.astype(BF16)


def density_kernel(inverse, sign, inv_tiles, out, placed, sems, local_sem, *bufs):
    def buf(team, oy, oz):
        return bufs[team * SLOTS + oy * 4 + oz]

    row, col, y, z, device = places()
    core = row % 2
    partner = (row + 1 - 2 * core, col)
    across = ((row + 2 * core - 1 + TEAMS) % TEAMS, col)
    near = [device(1, 0), device(3, 0), device(0, 1), device(0, 3), partner, across]
    for ref in bufs:
        ref[MEMBERS] = jnp.zeros((BLOCK, OWN), BF16)
    load = pltpu.make_async_copy(sign, buf(0, 0, 0).at[pl.ds(0, MEMBERS)], local_sem)
    load.start()
    load.wait()
    greet(near)

    def plane(team, rows, first):
        return Gather(
            lambda oy, oz, start, size: buf(team, oy, oz).at[pl.ds(start, size)],
            rows,
            sems.at[0, pl.ds(first, 40)],
            sems.at[1, pl.ds(first, 40)],
            device,
        )

    def onward(team, oy, oz, start, size, n):
        return pltpu.make_async_remote_copy(
            src_ref=buf(0, oy, oz).at[pl.ds(start, size)],
            dst_ref=buf(team, oy, oz).at[pl.ds(start, size)],
            send_sem=sems.at[0, n],
            recv_sem=sems.at[1, n],
            device_id=partner if team == 1 else across,
            device_id_type=MESH,
        )

    def to_partner(oy, oz):
        return onward(1, oy, oz, 0, MEMBERS, 80 + oy * 4 + oz)

    def to_across(oy, oz):
        return onward(2, oy, oz, SHARED, MEMBERS - SHARED, 96 + oy * 4 + oz)

    shared = onward(2, 0, 0, 0, SHARED, 112)
    shared.start()
    mine = plane(0, MEMBERS, 0)
    mine.begin()
    to_across(0, 0).start()
    to_partner(0, 0).start()
    shared.wait_recv()
    theirs = plane(2, SHARED, 40)
    theirs.begin()

    sides = [1, 2 - 2 * core, 2 * core]
    teams = [row, partner[0], across[0]]

    def multiply(team, pair):
        for t, (oy, oz) in enumerate(pair):
            slot = ((y + oy) % 4) * 4 + (z + oz) % 4
            line = teams[team] * SLOTS + slot

            @pl.loop(0, TEAM_BLOCKS // 8)
            def _(i):
                for j in range(8):
                    b = i * 8 + j
                    placed[pl.ds(pl.multiple_of(b * BLOCK, BLOCK), BLOCK), t * OWN : (t + 1) * OWN] = buf(
                        team, oy, oz
                    )[inverse[line, b]]

        side = sides[team]
        result = jnp.dot(inv_tiles[side], placed[...], preferred_element_type=F32)
        for t, (oy, oz) in enumerate(pair):
            slot = ((y + oy) % 4) * 4 + (z + oz) % 4
            out[side, :, pl.ds(pl.multiple_of(slot * OWN, OWN), OWN)] = result[:, t * OWN : (t + 1) * OWN]

    order, order_theirs, ready = [(0, 0)], [(0, 0)], []
    mine_steps, their_steps = mine.steps(), theirs.steps()
    turns = ["mine"] * LEAD + ["theirs", "mine"] * (40 - LEAD) + ["theirs"] * LEAD
    for turn in turns:
        if turn == "mine":
            spot = next(mine_steps)
            if spot:
                order.append(spot)
                to_across(*spot).start()
                to_partner(*spot).start()
                if len(order) % 2 == 0:
                    multiply(0, order[-2:])
                    ready.append(order[-2:])
        else:
            spot = next(their_steps)
            if spot:
                order_theirs.append(spot)
                if len(ready) > 1 or (ready and len(order) == SLOTS):
                    pair = ready.pop(0)
                    for spot in pair:
                        to_partner(*spot).wait_recv()
                    multiply(1, pair)
                if len(order_theirs) % 2 == 0:
                    for spot in order_theirs[-2:]:
                        to_across(*spot).wait_recv()
                    multiply(2, order_theirs[-2:])
    for pair in ready:
        for spot in pair:
            to_partner(*spot).wait_recv()
        multiply(1, pair)
    for last in (mine_steps, their_steps):
        assert next(last, None) is None
    shared.wait_send()
    mine.finish()
    theirs.finish()
    for spot in order:
        to_partner(*spot).wait_send()
        to_across(*spot).wait_send()


def shards(hamiltonian, pattern, onsite, members, orders, intersection_inv):
    smem = pl.BlockSpec(memory_space=pltpu.SMEM)
    vmem = pl.BlockSpec(memory_space=pltpu.VMEM)
    hits = members[:, None, :] == jnp.arange(TEAM_BLOCKS, dtype=jnp.int32)[None, :, None]
    behind = MEMBERS - jnp.arange(MEMBERS, dtype=jnp.int32)
    inverse = MEMBERS - jnp.sum(jnp.where(hits, behind, 0), axis=2)
    row, col = lax.axis_index("row"), lax.axis_index("col")
    group = lax.dynamic_index_in_dim(members, row * SLOTS + col, 0, keepdims=False)
    order = lax.dynamic_index_in_dim(orders, row * SLOTS + col, 0, keepdims=False)
    at = jnp.arange(MEMBERS, dtype=jnp.int32)
    part = group % OWN_BLOCKS
    slot = ((group // 16 - col // 4) % 4) * 4 + (group // OWN_BLOCKS - col) % 4
    turn = (at - part) % 4
    table = jnp.stack([group, slot * 4 + turn, slot, turn * SLOTS + group // OWN_BLOCKS, part])
    active = jnp.stack([(at < order).astype(F32), jnp.full((MEMBERS,), BLOCK, F32) * order.astype(F32)])
    sign = pl.pallas_call(
        sign_kernel,
        out_shape=jax.ShapeDtypeStruct((SUB, OWN), BF16),
        in_specs=[smem, smem, vmem, vmem, vmem],
        out_specs=vmem,
        scratch_shapes=[
            pltpu.VMEM((TEAM_BLOCKS, BLOCK, OWN), F32),
            pltpu.VMEM((4 * SLOTS, 1, OWN), F32),
            pltpu.VMEM((OWN, SUB), F32),
            pltpu.VMEM((SLOTS * 4, TILES, OWN, OWN), BF16),
            pltpu.VMEM((SLOTS, TILES, OWN_BLOCKS, BLOCK, OWN), BF16),
            pltpu.VMEM((SUB, SUB), BF16),
            pltpu.VMEM((1, SUB), F32),
            pltpu.SemaphoreType.DMA((40,)),
            pltpu.SemaphoreType.DMA((40,)),
            *[pltpu.VMEM((TEAM_BLOCKS, BLOCK, OWN), BF16) for _ in range(SLOTS)],
        ],
        compiler_params=pltpu.CompilerParams(
            collective_id=0, has_side_effects=True, vmem_limit_bytes=46 * 1024 * 1024
        ),
        name="sign_step",
    )(table, active, hamiltonian.reshape(TEAM_WIDTH, OWN), pattern.T, onsite.reshape(SLOTS, OWN))
    density = pl.pallas_call(
        density_kernel,
        out_shape=pltpu.VMEM((3, OWN, TEAM_WIDTH), F32),
        in_specs=[smem, pl.BlockSpec(memory_space=pl.ANY), vmem],
        out_specs=vmem,
        scratch_shapes=[
            pltpu.VMEM((TEAM_WIDTH, 2 * OWN), BF16),
            pltpu.SemaphoreType.DMA((2, 113)),
            pltpu.SemaphoreType.DMA,
            *[pltpu.VMEM((MEMBERS + 1, BLOCK, OWN), BF16) for _ in range(3 * SLOTS)],
        ],
        compiler_params=pltpu.CompilerParams(
            collective_id=1, has_side_effects=True, vmem_limit_bytes=40 * 1024 * 1024
        ),
        name="density",
    )(inverse, sign.reshape(MEMBERS, BLOCK, OWN), intersection_inv.transpose(1, 0, 2))
    return density.transpose(1, 0, 2)


def solution(mesh):
    in_specs = (P("row", "col"), P("row", "col"), P("row"), P(), P(), P(("row", "col"), None, None))
    out_specs = P(("row", "col"), None, None)
    return jax.shard_map(shards, mesh=mesh, in_specs=in_specs, out_specs=out_specs, check_vma=False)
```

profile of v0, /device:TPU:1, one launch (start us, length us, event | category | flops | bytes accessed | tf_op | source)
XLA Modules:
  0.0 121.7 jit_solution(6666627501617995552)
XLA Ops:
  0.0 1.2 %dynamic_slice.9 = s32[1]{0:T(128)} dynamic-slice(s32[128]{0:T(128)} %param.10, s32[]{:T(128)S(6)} %select_n.57), dynamic_slice_sizes={1} | dynamic-slice | bytes 12 | tf_op jit(solution)/shard_map/jit(dynamic_index_in_dim)/dynamic_slice | solution.py:343
  1.9 0.7 compare_convert_fusion
  2.6 0.8 constant_dynamic-slice_fusion
  3.4 0.1 copy.14
  3.5 0.9 select_reduce_fusion
  4.5 0.1 copy.12
  4.6 0.0 copy-start.1
  4.6 1.2 copy-done.1
  5.8 0.0 copy-start.2
  5.8 0.7 copy-done.2
  6.5 0.0 copy-start.3
  6.5 0.7 copy-done.3
  7.2 60.9 %sign_step.1 = bf16[1024,128]{1,0:T(8,128)(2,1)S(1)} custom-call(s32[5,32]{1,0:T(8,128)S(1)} %stack.4.table, f32[2,32]{1,0:T(2,128)S(1)} %stack.5.active, f32[2048,128]{1,0:T(8,128)S(1)} %copy-done.1, s32[4,64]{1,0:T(4,128)S(1)} %bitcast.10, f32[16,128]{1,0:T(8,128)S(1)} %bitcast.9), custom_call_target="tpu_custom_call" | custom-call | tf_op jit(solution)/shard_map/sign_step/pallas_call | solution.py:350
  68.1 0.0 copy-start
  68.1 1.4 %copy-done = bf16[128,3,2048]{2,0,1:T(8,128)(2,1)S(1)} copy-done((bf16[128,3,2048]{2,0,1:T(8,128)(2,1)S(1)}, bf16[128,3,2048]{2,0,1:T(8,128)(2,1)}, u32[]{:S(2)}) %copy-start) | copy-done | bytes 1572888
  69.5 50.5 %density.1 = f32[3,128,2048]{2,1,0:T(8,128)S(1)} custom-call(s32[128,64]{1,0:T(8,128)S(1)} %broadcast_subtract_fusion.inverse, bf16[32,32,128]{2,1,0:T(8,128)(2,1)S(1)} %bitcast.8, bf16[3,128,2048]{2,1,0:T(8,128)(2,1)S(1)} %bitcast.7), custom_call_target="tpu_custom_call" | custom-call | tf_op jit(solution)/shard_map/density/pallas_call | solution.py:372
  120.0 1.7 %copy.16 = f32[128,3,2048]{2,0,1:T(8,128)} copy(f32[128,3,2048]{2,0,1:T(8,128)S(1)} %bitcast.6) | data formatting | bytes 6291456
  (6 shorter events, 0.1 us)
Async XLA Ops:
  4.6 1.2 %copy-start.1 = (f32[2048,128]{1,0:T(8,128)S(1)}, f32[2048,128]{1,0:T(8,128)}, u32[]{:S(2)}) copy-start(f32[2048,128]{1,0:T(8,128)} %ham.1) | copy-start | bytes 3145732
  5.8 0.7 copy-start.2
  6.5 0.7 copy-start.3
  68.1 1.4 %copy-start = (bf16[128,3,2048]{2,0,1:T(8,128)(2,1)S(1)}, bf16[128,3,2048]{2,0,1:T(8,128)(2,1)}, u32[]{:S(2)}) copy-start(bf16[128,3,2048]{2,0,1:T(8,128)(2,1)} %param.11) | copy-start | bytes 4718596
where the time goes:
time: 122 us
  Pallas kernels  111 us (91%)
  local copies, waits for them, and re-layouts  7.9 us (6%)
  other arithmetic  1.66 us (1%)
    pallas_call x1, Pallas kernels, shards(): pl.pallas_call(sign_kernel, out_shape=jax.ShapeDtypeStruct((SUB, OWN), BF...  60.9 us
    pallas_call x1, Pallas kernels, shards(): pl.pallas_call(density_kernel, out_shape=pltpu.VMEM((3, OWN, TEAM_WIDTH),...  50.5 us
    unnamed x10, local copies, waits for them, and re-layouts  5.75 us

commit v1 on v0

v1 whole, which is shorter than its diff:
```python
import jax
import jax.numpy as jnp
from jax import lax
from jax.experimental import pallas as pl
from jax.experimental.pallas import tpu as pltpu
from jax.sharding import PartitionSpec as P

BLOCK = 32
OWN_BLOCKS = 4
MEMBERS = 32
SLOTS = 16
TEAMS = 8
TEAM_BLOCKS = 64
TEAM_WIDTH = 2048
SUB = MEMBERS * BLOCK
OWN = OWN_BLOCKS * BLOCK
TILES = SUB // OWN
F32 = jnp.float32
BF16 = jnp.bfloat16
MESH = pl.DeviceIdType.MESH
SHARED = 12
LEAD = 10
RINGS = ((0, 0), (0, 1), (1, 0), (1, 1), (0, 2), (0, 3), (4, 0), (4, 1), (2, 0), (2, 1))
RINGS += ((1, 2), (1, 3), (3, 0), (3, 1), (4, 2), (4, 3), (2, 2), (2, 3), (3, 2), (3, 3))
FIRST = [half * 20 + ring * 4 + k for ring, k in RINGS for half in (0, 1)]
SECOND = FIRST[:LEAD]
for lag in range(40 - LEAD):
    SECOND += [40 + FIRST[lag], FIRST[LEAD + lag]]
SECOND += [40 + n for n in FIRST[40 - LEAD :]]
RING_K = ((0, 3), (0, 1), (3, 2), (1, 2))


class Gather:
    def __init__(self, region, rows, send_sems, recv_sems, device):
        self.region, self.rows, self.device = region, rows, device
        self.send_sems, self.recv_sems = send_sems, recv_sems
        self.got, self.seen = {(0, 0): {0, 1}}, set()

    def copy(self, half, ring, k):
        source, landing = RING_K[k]
        step = 1 if k in (0, 2) else -1
        rows = self.rows // 2
        start, size = half * rows, rows
        if k >= 2:
            size = rows // 2
            start += size * (k - 2)

        def spot(offset):
            a, b = (offset, 0) if ring == 0 else (ring - 1, offset)
            return (b, a) if half == 0 else (a, b)

        along_z = (half == 0) == (ring == 0)
        n = half * 20 + ring * 4 + k
        return pltpu.make_async_remote_copy(
            src_ref=self.region(*spot(source), start, size),
            dst_ref=self.region(*spot(landing), start, size),
            send_sem=self.send_sems.at[n],
            recv_sem=self.recv_sems.at[n],
            device_id=self.device(0, step) if along_z else self.device(step, 0),
            device_id_type=MESH,
        ), spot(landing)

    def begin(self):
        for ring in (0, 1):
            for half in (0, 1):
                for k in (0, 1):
                    self.copy(half, ring, k)[0].start()

    def arrive(self, half, ring, k):
        copy, spot = self.copy(half, ring, k)
        copy.wait_recv()
        if k < 2:
            self.copy(half, ring, k + 2)[0].start()
        self.seen.add((half, ring, k))
        if k >= 2 and (half, ring, 5 - k) not in self.seen:
            return None, False
        if ring == 0:
            for j in (0, 1):
                self.copy(half, RING_K[k][1] + 1, j)[0].start()
        halves = self.got.setdefault(spot, set())
        halves.add(half)
        return spot, len(halves) == 2

    def finish(self):
        for half in (0, 1):
            for ring in range(5):
                for k in range(4):
                    self.copy(half, ring, k)[0].wait_send()


def places():
    row, col = lax.axis_index("row"), lax.axis_index("col")
    y, z = col // 4, col % 4

    def device(dy, dz):
        return (row, ((y + dy + 4) % 4) * 4 + (z + dz + 4) % 4)

    return row, col, y, z, device


def kernel(
    table, active, inverse, ham_in, pattern, onsite, inv_in, out,
    ham, inv_tiles, own, onsites, left, rolled, turned, mat, diag, placed, local_sems, sems, *scratch
):
    row, col, y, z, device = places()
    group = row * SLOTS + col
    core = row % 2
    partner = (row + 1 - 2 * core, col)
    across = ((row + 2 * core - 1 + TEAMS) % TEAMS, col)
    near = [device(1, 0), device(3, 0), device(0, 1), device(0, 3), partner, across]
    barrier = pltpu.get_barrier_semaphore()
    for one in near:
        pl.semaphore_signal(barrier, inc=1, device_id=one, device_id_type=MESH)
    ham_load = pltpu.make_async_copy(ham_in, ham, local_sems.at[0])
    inv_load = pltpu.make_async_copy(inv_in, inv_tiles, local_sems.at[1])
    ham_load.start()
    inv_load.start()
    bufs, signs = scratch[:SLOTS], scratch[SLOTS:]
    for ref in signs:
        ref[MEMBERS] = jnp.zeros((BLOCK, OWN), BF16)
    lanes = lax.broadcasted_iota(jnp.int32, (OWN_BLOCKS, OWN), 1) // BLOCK
    spread = (lanes == lax.broadcasted_iota(jnp.int32, (OWN_BLOCKS, OWN), 0)).astype(F32)
    weights = lax.dot_general(
        pattern[...].astype(F32), spread, (((0,), (0,)), ((), ())), preferred_element_type=F32
    )
    ham_load.wait()
    for a in range(TEAM_BLOCKS):
        masked = ham[a * BLOCK : (a + 1) * BLOCK, :] * weights[a : a + 1, :]
        own[a] = masked
        bufs[0][a] = masked.astype(BF16)
    pl.semaphore_wait(barrier, len(near))

    def plane(region, rows, first):
        return Gather(region, rows, sems.at[0, pl.ds(first, 40)], sems.at[1, pl.ds(first, 40)], device)

    gather = plane(lambda oy, oz, start, size: bufs[oy * 4 + oz].at[pl.ds(start, size)], TEAM_BLOCKS, 0)
    gather.begin()
    for s in range(4):
        onsites[s * SLOTS : (s + 1) * SLOTS] = pltpu.roll(onsite[...], s * BLOCK, axis=1).reshape(SLOTS, 1, OWN)
    one_row = lax.broadcasted_iota(jnp.int32, (1, OWN), 1) // BLOCK

    def blocks(read, tile):
        pieces = [read(table[0, tile * 4 + q, group]).astype(F32) * active[tile * 4 + q, group] for q in range(4)]
        return jnp.concatenate(pieces, axis=0)

    @pl.loop(0, TILES)
    def _(tile):
        at = pl.ds(pl.multiple_of(tile * OWN, OWN), OWN)
        left[:, at] = blocks(lambda m: own[m], tile).T
        picked = jnp.zeros((1, OWN), F32)
        for q in range(4):
            line = onsites[table[3, tile * 4 + q, group]] * active[tile * 4 + q, group]
            picked = jnp.where(one_row == q, line, picked)
        diag[:, at] = picked

    def take_in(oy, oz):
        slot = oy * 4 + oz

        @pl.loop(0, TILES)
        def _(tile):
            x = blocks(lambda m: bufs[slot][m], tile)
            turned[slot, tile] = x.T.astype(BF16).reshape(4, BLOCK, OWN)
            rolled[slot * 4, tile] = x.astype(BF16)
            for s in (1, 2, 3):
                rolled[slot * 4 + s, tile] = pltpu.roll(x, s * BLOCK, axis=1).astype(BF16)

    take_in(0, 0)
    for n in FIRST:
        spot, whole = gather.arrive(n // 20, n % 20 // 4, n % 4)
        if whole:
            take_in(*spot)

    which = lax.broadcasted_iota(jnp.int32, (OWN, OWN), 1) // BLOCK
    eye = lax.broadcasted_iota(jnp.int32, (OWN, OWN), 0) == lax.broadcasted_iota(jnp.int32, (OWN, OWN), 1)

    def direct(up, over):
        tile = None
        for q in range(4):
            piece = rolled[table[1, over * 4 + q, group], up].astype(F32) * active[over * 4 + q, group]
            tile = piece if tile is None else jnp.where(which == q, piece, tile)
        return tile

    def mirrored(up, over):
        pieces = []
        for q in range(4):
            a = up * 4 + q
            pieces.append(turned[table[2, a, group], over, table[4, a, group]].astype(F32) * active[a, group])
        return jnp.concatenate(pieces, axis=0)

    def assemble(n, total):
        up, over = n // TILES, n % TILES
        tile = 0.5 * (direct(up, over) + mirrored(up, over))
        mat[pl.ds(pl.multiple_of(up * OWN, OWN), OWN), pl.ds(pl.multiple_of(over * OWN, OWN), OWN)] = tile.astype(
            BF16
        )
        return total + jnp.sum((tile * tile).reshape(OWN // 8, 8, OWN), axis=0)

    total = lax.fori_loop(0, TILES * TILES, assemble, jnp.zeros((8, OWN), F32))

    extra = jnp.zeros((1, OWN), F32)
    start = []
    for tile in range(TILES):
        at = slice(tile * OWN, (tile + 1) * OWN)
        on_diag = jnp.sum(jnp.where(eye, mat[at, at].astype(F32), 0.0), axis=0, keepdims=True)
        energy = diag[:, at]
        extra += energy * (2.0 * on_diag + energy)
        first = 0.5 * (left[:, at] + direct(0, tile))
        if tile == 0:
            first += jnp.where(eye, energy, 0.0)
        start.append(first)
    count = 0.0
    for a in range(MEMBERS):
        count += active[a, group] * float(BLOCK)
    squares = jnp.sum(jnp.sum(total, axis=0, keepdims=True) + extra, axis=1, keepdims=True)
    scale = jnp.sqrt(count / (4.0 * (squares + 1e-06)))
    energy = diag[...]

    def apply(x):
        high = x.astype(BF16)
        low = (x - high.astype(F32)).astype(BF16)
        y = jnp.dot(jnp.concatenate([high, low], axis=0), mat[...], preferred_element_type=F32)
        return scale * (y[:OWN] + y[OWN:] + x * energy)

    initial = scale * jnp.concatenate(start, axis=1)
    first_step = 1.5 * initial - 0.5 * apply(apply(initial))
    once = apply(first_step)
    once = 1.5 * once - 0.5 * apply(apply(once))
    twice = apply(once)
    twice = 1.5 * twice - 0.5 * apply(apply(twice))
    result = 1.5 * first_step - 0.5 * twice
    for tile in range(TILES):
        turned_back = result[:, tile * OWN : (tile + 1) * OWN].T.astype(BF16)
        signs[0][tile * 4 : (tile + 1) * 4] = turned_back.reshape(4, BLOCK, OWN)
    gather.finish()
    inv_load.wait()

    def sign_at(team, oy, oz):
        return signs[team * SLOTS + oy * 4 + oz]

    def onward(team, oy, oz, start, size, n):
        return pltpu.make_async_remote_copy(
            src_ref=sign_at(0, oy, oz).at[pl.ds(start, size)],
            dst_ref=sign_at(team, oy, oz).at[pl.ds(start, size)],
            send_sem=sems.at[0, n],
            recv_sem=sems.at[1, n],
            device_id=partner if team == 1 else across,
            device_id_type=MESH,
        )

    def to_partner(oy, oz):
        return onward(1, oy, oz, 0, MEMBERS, 120 + oy * 4 + oz)

    def to_across(oy, oz, half):
        start = half * MEMBERS // 2 + SHARED // 2
        return onward(2, oy, oz, start, (MEMBERS - SHARED) // 2, 136 + half * SLOTS + oy * 4 + oz)

    shared = [onward(2, 0, 0, half * MEMBERS // 2, SHARED // 2, 168 + half) for half in (0, 1)]
    for half in (0, 1):
        shared[half].start()
    mine = plane(lambda oy, oz, start, size: sign_at(0, oy, oz).at[pl.ds(start, size)], MEMBERS, 40)
    mine.begin()
    for half in (0, 1):
        to_across(0, 0, half).start()
    to_partner(0, 0).start()
    for half in (0, 1):
        shared[half].wait_recv()

    def shared_part(oy, oz, start, size):
        half = start // (SHARED // 2)
        return sign_at(2, oy, oz).at[pl.ds(half * MEMBERS // 2 + start % (SHARED // 2), size)]

    theirs = plane(shared_part, SHARED, 80)
    theirs.begin()

    sides = [1, 2 - 2 * core, 2 * core]
    teams = [row, partner[0], across[0]]

    def multiply(team, pair):
        for t, (oy, oz) in enumerate(pair):
            slot = ((y + oy) % 4) * 4 + (z + oz) % 4
            line = teams[team] * SLOTS + slot

            @pl.loop(0, TEAM_BLOCKS // 8)
            def _(i):
                for j in range(8):
                    b = i * 8 + j
                    placed[pl.ds(pl.multiple_of(b * BLOCK, BLOCK), BLOCK), t * OWN : (t + 1) * OWN] = sign_at(
                        team, oy, oz
                    )[inverse[line, b]]

        side = sides[team]
        result = jnp.dot(inv_tiles[side], placed[...], preferred_element_type=F32)
        for t, (oy, oz) in enumerate(pair):
            slot = ((y + oy) % 4) * 4 + (z + oz) % 4
            out[side, :, pl.ds(pl.multiple_of(slot * OWN, OWN), OWN)] = result[:, t * OWN : (t + 1) * OWN]

    order, order_theirs, ready = [(0, 0)], [(0, 0)], []
    for n in SECOND:
        half, ring, k = n % 40 // 20, n % 20 // 4, n % 4
        spot, whole = (mine if n < 40 else theirs).arrive(half, ring, k)
        if n < 40 and spot:
            to_across(*spot, half).start()
        if not whole:
            continue
        if n < 40:
            order.append(spot)
            to_partner(*spot).start()
            if len(order) % 2 == 0:
                multiply(0, order[-2:])
                ready.append(order[-2:])
        else:
            order_theirs.append(spot)
            if len(ready) > 1 or (ready and len(order) == SLOTS):
                pair = ready.pop(0)
                for one in pair:
                    to_partner(*one).wait_recv()
                multiply(1, pair)
            if len(order_theirs) % 2 == 0:
                for one in order_theirs[-2:]:
                    to_across(*one, 0).wait_recv()
                    to_across(*one, 1).wait_recv()
                multiply(2, order_theirs[-2:])
    for pair in ready:
        for one in pair:
            to_partner(*one).wait_recv()
        multiply(1, pair)
    mine.finish()
    theirs.finish()
    for half in (0, 1):
        shared[half].wait_send()
        for one in order:
            to_across(*one, half).wait_send()
    for one in order:
        to_partner(*one).wait_send()


def shards(hamiltonian, pattern, onsite, members, orders, intersection_inv):
    smem = pl.BlockSpec(memory_space=pltpu.SMEM)
    vmem = pl.BlockSpec(memory_space=pltpu.VMEM)
    hbm = pl.BlockSpec(memory_space=pl.ANY)
    across = members.T
    hits = across[:, :, None] == jnp.arange(TEAM_BLOCKS, dtype=jnp.int32)
    behind = MEMBERS - jnp.arange(MEMBERS, dtype=jnp.int32)
    inverse = MEMBERS - jnp.sum(jnp.where(hits, behind[:, None, None], 0), axis=0)
    col = lax.axis_index("col")
    which = lax.broadcasted_iota(jnp.int32, (5, MEMBERS, TEAMS * SLOTS), 0)
    at = lax.broadcasted_iota(jnp.int32, (MEMBERS, TEAMS * SLOTS), 0)
    part, block = across & 3, across >> 2
    slot = (((block >> 2) - (col >> 2)) & 3) * 4 + ((block - col) & 3)
    turn = (at - part) & 3
    table = part
    for n, values in enumerate((across, slot * 4 + turn, slot, turn * SLOTS + block)):
        table = jnp.where(which == n, values, table)
    active = (at < orders).astype(F32)
    density = pl.pallas_call(
        kernel,
        out_shape=pltpu.VMEM((3, OWN, TEAM_WIDTH), F32),
        in_specs=[smem, smem, smem, hbm, vmem, vmem, hbm],
        out_specs=vmem,
        scratch_shapes=[
            pltpu.VMEM((TEAM_WIDTH, OWN), F32),
            pltpu.VMEM((3, OWN, TEAM_WIDTH), BF16),
            pltpu.VMEM((TEAM_BLOCKS, BLOCK, OWN), F32),
            pltpu.VMEM((4 * SLOTS, 1, OWN), F32),
            pltpu.VMEM((OWN, SUB), F32),
            pltpu.VMEM((SLOTS * 4, TILES, OWN, OWN), BF16),
            pltpu.VMEM((SLOTS, TILES, OWN_BLOCKS, BLOCK, OWN), BF16),
            pltpu.VMEM((SUB, SUB), BF16),
            pltpu.VMEM((1, SUB), F32),
            pltpu.VMEM((TEAM_WIDTH, 2 * OWN), BF16),
            pltpu.SemaphoreType.DMA((2,)),
            pltpu.SemaphoreType.DMA((2, 170)),
            *[pltpu.VMEM((TEAM_BLOCKS, BLOCK, OWN), BF16) for _ in range(SLOTS)],
            *[pltpu.VMEM((MEMBERS + 1, BLOCK, OWN), BF16) for _ in range(3 * SLOTS)],
        ],
        compiler_params=pltpu.CompilerParams(
            collective_id=0, has_side_effects=True, vmem_limit_bytes=56 * 1024 * 1024
        ),
        name="density",
    )(table, active, inverse, hamiltonian, pattern.T, onsite.reshape(SLOTS, OWN), intersection_inv.transpose(1, 0, 2))
    return density.transpose(1, 0, 2)


def solution(mesh):
    in_specs = (P("row", "col"), P("row", "col"), P("row"), P(), P(), P(("row", "col"), None, None))
    out_specs = P(("row", "col"), None, None)
    return jax.shard_map(shards, mesh=mesh, in_specs=in_specs, out_specs=out_specs, check_vma=False)
```

time: 122 us -> 115 us (0.943)
  local copies, waits for them, and re-layouts: 7.9 us -> 1.76 us
  Pallas kernels: 111 us -> 107 us
  other arithmetic: 1.66 us -> 4.98 us
    unnamed x10 -> x1, local copies, waits for them, and re-layouts: 5.75 us -> 1.67 us
    pallas_call x2 -> x1, Pallas kernels: 111 us -> 107 us  [shards(): pl.pallas_call(kernel, out_shape=pltpu.VMEM((3, OWN, TEAM_WIDTH), F32), i...]
    dynamic_slice x2 -> x0, local copies, waits for them, and re-layouts: 2.03 us -> none  [the longest x1 1.24 us: shards(): lax.dynamic_index_in_dim(orders, row * SLOTS + col, 0, keepdims=False)]
    select_n x0 -> x1, other arithmetic: none -> 1.45 us  [shards(): table = jnp.where(which == n, values, table)]
where the time goes in v1:
time: 115 us; the launch traced here: 114 us
  Pallas kernels  107 us (93%)
  other arithmetic  4.98 us (4%)
  local copies, waits for them, and re-layouts  1.76 us (2%)
    pallas_call x1, Pallas kernels, shards(): pl.pallas_call(kernel, out_shape=pltpu.VMEM((3, OWN, TEAM_WIDTH), F32), i...  107 us

profile of v1, /device:TPU:1, one launch (start us, length us, event | category | flops | bytes accessed | tf_op | source)
XLA Modules:
  0.0 114.2 jit_solution(9186537267831487240)
XLA Ops:
  0.0 1.3 %fusion.active = f32[32,128]{1,0:T(8,128)} fusion(s32[128]{0:T(128)} %param.10), kind=kLoop, calls=%fused_computation.9 | loop fusion | flops 8192 | bytes 16896 | tf_op jit(solution)/shard_map/convert_element_type | solution.py:354
  1.3 0.9 select_reduce_fusion
  2.2 0.1 copy.9
  2.3 0.6 broadcast_subtract_fusion.inverse
  2.9 0.7 multiply_add_fusion.1
  3.6 1.4 %select_select_fusion.table = s32[5,32,128]{2,1,0:T(8,128)} fusion(s32[32,128]{1,0:T(8,128)S(1)} %get-tuple-element.6, s32[32,128]{1,0:T(8,128)} %bitcast.14, s32[32,128]{1,0:T(8,128)S(1)} %get-tuple-element.8, s32[32,128]{1,0:T(8,128)S(1)} %get-tuple-element.7, s32[32,128]{1,0:T(8,128)S(1)} %get-tuple-element.5, pred[5]{0:T(512)(128)(4,1)S(1)} %get-tuple-element.9, ...), kind=kLoop, calls=%fused_computation.2 | loop fusion | flops 81920 | bytes 163860 | tf_op jit(solution)/shard_map/jit(_where)/select_n | solution.py:353
  5.1 107.4 %density.1 = f32[3,128,2048]{2,1,0:T(8,128)S(1)} custom-call(s32[5,32,128]{2,1,0:T(8,128)} %select_select_fusion.table, f32[32,128]{1,0:T(8,128)} %fusion.active, s32[128,64]{1,0:T(8,128)} %broadcast_subtract_fusion.inverse, f32[2048,128]{1,0:T(8,128)} %ham_in.1, s32[4,64]{1,0:T(4,128)} %bitcast.16, f32[16,128]{1,0:T(8,128)} %bitcast.15, ...), custom_call_target="tpu_custom_call" | custom-call | tf_op jit(solution)/shard_map/density/pallas_call | solution.py:355
  112.5 1.7 %copy.11 = f32[128,3,2048]{2,0,1:T(8,128)} copy(f32[128,3,2048]{2,0,1:T(8,128)S(1)} %bitcast.11) | data formatting | bytes 6291456
  (3 shorter events, 0.0 us)

commit v2 on v1

--- a/solution.py
+++ b/solution.py
@@ -20,6 +20,8 @@
 MESH = pl.DeviceIdType.MESH
 SHARED = 12
 LEAD = 10
+LAG = 4
+UNITS = 1
 RINGS = ((0, 0), (0, 1), (1, 0), (1, 1), (0, 2), (0, 3), (4, 0), (4, 1), (2, 0), (2, 1))
 RINGS += ((1, 2), (1, 3), (3, 0), (3, 1), (4, 2), (4, 3), (2, 2), (2, 3), (3, 2), (3, 3))
 FIRST = [half * 20 + ring * 4 + k for ring, k in RINGS for half in (0, 1)]
@@ -99,7 +101,7 @@
 
 
 def kernel(
-    table, active, inverse, ham_in, pattern, onsite, inv_in, out,
+    listed, rolled_at, slot_at, onsite_at, part_at, active, inverse, ham_in, pattern, onsite, inv_in, out,
     ham, inv_tiles, own, onsites, left, rolled, turned, mat, diag, placed, local_sems, sems, *scratch
 ):
     row, col, y, z, device = places()
@@ -117,7 +119,7 @@
     inv_load.start()
     bufs, signs = scratch[:SLOTS], scratch[SLOTS:]
     for ref in signs:
-        ref[MEMBERS] = jnp.zeros((BLOCK, OWN), BF16)
+        ref[0] = jnp.zeros((BLOCK, OWN), BF16)
     lanes = lax.broadcasted_iota(jnp.int32, (OWN_BLOCKS, OWN), 1) // BLOCK
     spread = (lanes == lax.broadcasted_iota(jnp.int32, (OWN_BLOCKS, OWN), 0)).astype(F32)
     weights = lax.dot_general(
@@ -140,7 +142,7 @@
     one_row = lax.broadcasted_iota(jnp.int32, (1, OWN), 1) // BLOCK
 
     def blocks(read, tile):
-        pieces = [read(table[0, tile * 4 + q, group]).astype(F32) * active[tile * 4 + q, group] for q in range(4)]
+        pieces = [read(listed[tile * 4 + q, group]).astype(F32) * active[tile * 4 + q, group] for q in range(4)]
         return jnp.concatenate(pieces, axis=0)
 
     @pl.loop(0, TILES)
@@ -149,7 +151,7 @@
         left[:, at] = blocks(lambda m: own[m], tile).T
         picked = jnp.zeros((1, OWN), F32)
         for q in range(4):
-            line = onsites[table[3, tile * 4 + q, group]] * active[tile * 4 + q, group]
+            line = onsites[onsite_at[tile * 4 + q, group]] * active[tile * 4 + q, group]
             picked = jnp.where(one_row == q, line, picked)
         diag[:, at] = picked
 
@@ -176,7 +178,7 @@
     def direct(up, over):
         tile = None
         for q in range(4):
-            piece = rolled[table[1, over * 4 + q, group], up].astype(F32) * active[over * 4 + q, group]
+            piece = rolled[rolled_at[over * 4 + q, group], up].astype(F32) * active[over * 4 + q, group]
             tile = piece if tile is None else jnp.where(which == q, piece, tile)
         return tile
 
@@ -184,7 +186,7 @@
         pieces = []
         for q in range(4):
             a = up * 4 + q
-            pieces.append(turned[table[2, a, group], over, table[4, a, group]].astype(F32) * active[a, group])
+            pieces.append(turned[slot_at[a, group], over, part_at[a, group]].astype(F32) * active[a, group])
         return jnp.concatenate(pieces, axis=0)
 
     def assemble(n, total):
@@ -230,7 +232,7 @@
     result = 1.5 * first_step - 0.5 * twice
     for tile in range(TILES):
         turned_back = result[:, tile * OWN : (tile + 1) * OWN].T.astype(BF16)
-        signs[0][tile * 4 : (tile + 1) * 4] = turned_back.reshape(4, BLOCK, OWN)
+        signs[0][tile * 4 + 1 : tile * 4 + 5] = turned_back.reshape(4, BLOCK, OWN)
     gather.finish()
     inv_load.wait()
 
@@ -239,8 +241,8 @@
 
     def onward(team, oy, oz, start, size, n):
         return pltpu.make_async_remote_copy(
-            src_ref=sign_at(0, oy, oz).at[pl.ds(start, size)],
-            dst_ref=sign_at(team, oy, oz).at[pl.ds(start, size)],
+            src_ref=sign_at(0, oy, oz).at[pl.ds(start + 1, size)],
+            dst_ref=sign_at(team, oy, oz).at[pl.ds(start + 1, size)],
             send_sem=sems.at[0, n],
             recv_sem=sems.at[1, n],
             device_id=partner if team == 1 else across,
@@ -257,7 +259,7 @@
     shared = [onward(2, 0, 0, half * MEMBERS // 2, SHARED // 2, 168 + half) for half in (0, 1)]
     for half in (0, 1):
         shared[half].start()
-    mine = plane(lambda oy, oz, start, size: sign_at(0, oy, oz).at[pl.ds(start, size)], MEMBERS, 40)
+    mine = plane(lambda oy, oz, start, size: sign_at(0, oy, oz).at[pl.ds(start + 1, size)], MEMBERS, 40)
     mine.begin()
     for half in (0, 1):
         to_across(0, 0, half).start()
@@ -267,7 +269,7 @@
 
     def shared_part(oy, oz, start, size):
         half = start // (SHARED // 2)
-        return sign_at(2, oy, oz).at[pl.ds(half * MEMBERS // 2 + start % (SHARED // 2), size)]
+        return sign_at(2, oy, oz).at[pl.ds(half * MEMBERS // 2 + start % (SHARED // 2) + 1, size)]
 
     theirs = plane(shared_part, SHARED, 80)
     theirs.begin()
@@ -275,55 +277,64 @@
     sides = [1, 2 - 2 * core, 2 * core]
     teams = [row, partner[0], across[0]]
 
+    def place(team, spot, t):
+        slot = ((y + spot[0]) % 4) * 4 + (z + spot[1]) % 4
+        line = teams[team] * SLOTS + slot
+
+        @pl.loop(0, TEAM_BLOCKS // 16)
+        def _(i):
+            for j in range(16):
+                b = i * 16 + j
+                rows = pl.ds(pl.multiple_of(b * BLOCK, BLOCK), BLOCK)
+                placed[rows, t * OWN : (t + 1) * OWN] = sign_at(team, *spot)[inverse[b, line]]
+
     def multiply(team, pair):
-        for t, (oy, oz) in enumerate(pair):
-            slot = ((y + oy) % 4) * 4 + (z + oz) % 4
-            line = teams[team] * SLOTS + slot
-
-            @pl.loop(0, TEAM_BLOCKS // 8)
-            def _(i):
-                for j in range(8):
-                    b = i * 8 + j
-                    placed[pl.ds(pl.multiple_of(b * BLOCK, BLOCK), BLOCK), t * OWN : (t + 1) * OWN] = sign_at(
-                        team, oy, oz
-                    )[inverse[line, b]]
-
         side = sides[team]
         result = jnp.dot(inv_tiles[side], placed[...], preferred_element_type=F32)
         for t, (oy, oz) in enumerate(pair):
             slot = ((y + oy) % 4) * 4 + (z + oz) % 4
             out[side, :, pl.ds(pl.multiple_of(slot * OWN, OWN), OWN)] = result[:, t * OWN : (t + 1) * OWN]
 
-    order, order_theirs, ready = [(0, 0)], [(0, 0)], []
+    def work(team, pair):
+        for t, spot in enumerate(pair):
+            if team == 1:
+                to_partner(*spot).wait_recv()
+            if team == 2:
+                to_across(*spot, 0).wait_recv()
+                to_across(*spot, 1).wait_recv()
+            place(team, spot, t)
+            yield
+        multiply(team, pair)
+        yield
+
+    order, order_theirs, todo = [(0, 0)], [(0, 0)], []
     for n in SECOND:
         half, ring, k = n % 40 // 20, n % 20 // 4, n % 4
         spot, whole = (mine if n < 40 else theirs).arrive(half, ring, k)
         if n < 40 and spot:
             to_across(*spot, half).start()
-        if not whole:
-            continue
-        if n < 40:
+        if n < 40 and whole:
             order.append(spot)
             to_partner(*spot).start()
             if len(order) % 2 == 0:
-                multiply(0, order[-2:])
-                ready.append(order[-2:])
-        else:
+                todo.append(work(0, order[-2:]))
+                if len(order) > 2:
+                    todo.append(work(1, order[-4:-2]))
+            if len(order) == SLOTS:
+                todo.append(work(1, order[-2:]))
+        if n >= 40 and whole:
             order_theirs.append(spot)
-            if len(ready) > 1 or (ready and len(order) == SLOTS):
-                pair = ready.pop(0)
-                for one in pair:
-                    to_partner(*one).wait_recv()
-                multiply(1, pair)
-            if len(order_theirs) % 2 == 0:
-                for one in order_theirs[-2:]:
-                    to_across(*one, 0).wait_recv()
-                    to_across(*one, 1).wait_recv()
-                multiply(2, order_theirs[-2:])
-    for pair in ready:
-        for one in pair:
-            to_partner(*one).wait_recv()
-        multiply(1, pair)
+            at = len(order_theirs) - LAG
+            if at > 0 and at % 2 == 0:
+                todo.append(work(2, order_theirs[at - 2 : at]))
+        for _ in range(UNITS):
+            while todo and next(todo[0], "end") == "end":
+                todo.pop(0)
+    for at in range(SLOTS - LAG, SLOTS, 2):
+        todo.append(work(2, order_theirs[at : at + 2]))
+    for steps in todo:
+        for _ in steps:
+            pass
     mine.finish()
     theirs.finish()
     for half in (0, 1):
@@ -338,24 +349,20 @@
     smem = pl.BlockSpec(memory_space=pltpu.SMEM)
     vmem = pl.BlockSpec(memory_space=pltpu.VMEM)
     hbm = pl.BlockSpec(memory_space=pl.ANY)
-    across = members.T
-    hits = across[:, :, None] == jnp.arange(TEAM_BLOCKS, dtype=jnp.int32)
-    behind = MEMBERS - jnp.arange(MEMBERS, dtype=jnp.int32)
-    inverse = MEMBERS - jnp.sum(jnp.where(hits, behind[:, None, None], 0), axis=0)
+    listed = members.T
+    places_of = lax.broadcasted_iota(jnp.int32, (MEMBERS, TEAM_BLOCKS, TEAMS * SLOTS), 0) + 1
+    hits = listed[:, None, :] == lax.broadcasted_iota(jnp.int32, places_of.shape, 1)
+    inverse = jnp.sum(jnp.where(hits, places_of, 0), axis=0)
     col = lax.axis_index("col")
-    which = lax.broadcasted_iota(jnp.int32, (5, MEMBERS, TEAMS * SLOTS), 0)
     at = lax.broadcasted_iota(jnp.int32, (MEMBERS, TEAMS * SLOTS), 0)
-    part, block = across & 3, across >> 2
+    part, block = listed & 3, listed >> 2
     slot = (((block >> 2) - (col >> 2)) & 3) * 4 + ((block - col) & 3)
     turn = (at - part) & 3
-    table = part
-    for n, values in enumerate((across, slot * 4 + turn, slot, turn * SLOTS + block)):
-        table = jnp.where(which == n, values, table)
     active = (at < orders).astype(F32)
     density = pl.pallas_call(
         kernel,
         out_shape=pltpu.VMEM((3, OWN, TEAM_WIDTH), F32),
-        in_specs=[smem, smem, smem, hbm, vmem, vmem, hbm],
+        in_specs=[smem] * 7 + [hbm, vmem, vmem, hbm],
         out_specs=vmem,
         scratch_shapes=[
             pltpu.VMEM((TEAM_WIDTH, OWN), F32),
@@ -377,7 +384,19 @@
             collective_id=0, has_side_effects=True, vmem_limit_bytes=56 * 1024 * 1024
         ),
         name="density",
-    )(table, active, inverse, hamiltonian, pattern.T, onsite.reshape(SLOTS, OWN), intersection_inv.transpose(1, 0, 2))
+    )(
+        listed,
+        slot * 4 + turn,
+        slot,
+        turn * SLOTS + block,
+        part,
+        active,
+        inverse,
+        hamiltonian,
+        pattern.T,
+        onsite.reshape(SLOTS, OWN),
+        intersection_inv.transpose(1, 0, 2),
+    )
     return density.transpose(1, 0, 2)
 
 

time: 115 us -> 113 us (0.983)
    select_n x1 -> x0, other arithmetic: 1.45 us -> none  [shards(): table = jnp.where(which == n, values, table)]
    and x0 -> x1, other arithmetic: none -> 1.35 us  [shards(): part, block = (listed & 3, listed >> 2)]
where the time goes in v2:
time: 113 us
  Pallas kernels  107 us (95%)
  other arithmetic  4.12 us (4%)
  local copies, waits for them, and re-layouts  1.67 us (1%)
    pallas_call x1, Pallas kernels, shards(): pl.pallas_call(kernel, out_shape=pltpu.VMEM((3, OWN, TEAM_WIDTH), F32), i...  107 us

profile of v2, /device:TPU:1, one launch (start us, length us, event | category | flops | bytes accessed | tf_op | source)
XLA Modules:
  0.0 112.6 jit_solution(5100149392576356684)
XLA Ops:
  0.0 1.3 %fusion.active = f32[32,128]{1,0:T(8,128)} fusion(s32[128]{0:T(128)} %param.10), kind=kLoop, calls=%fused_computation.7 | loop fusion | flops 8192 | bytes 16896 | tf_op jit(solution)/shard_map/convert_element_type | solution.py:361
  1.3 1.5 %select_reduce_fusion.inverse = s32[64,128]{1,0:T(8,128)} fusion(s32[32]{0:T(128)S(1)} %iota_add_fusion, s32[32,128]{1,0:T(8,128)} %bitcast.13), kind=kLoop, calls=%fused_computation | loop fusion | flops 778240 | bytes 49280 | tf_op jit(solution)/shard_map/reduce_sum | solution.py:355
  2.8 1.3 %broadcast_and_fusion = (s32[32,128]{1,0:T(8,128)}, s32[32,128]{1,0:T(8,128)}, s32[32,128]{1,0:T(8,128)}, s32[32,128]{1,0:T(8,128)}) fusion(s32[128,32]{0,1:T(8,128)} %param.9, s32[]{:T(128)S(6)} %axis_index.12, s32[]{:T(128)S(6)} %shift_right_arithmetic.11), kind=kLoop, calls=%fused_computation.8 | loop fusion | flops 61440 | bytes 81928 | tf_op jit(solution)/shard_map/and | solution.py:358
  4.1 106.8 %density.1 = f32[3,128,2048]{2,1,0:T(8,128)S(1)} custom-call(s32[32,128]{1,0:T(8,128)} %bitcast.14, s32[32,128]{1,0:T(8,128)} %get-tuple-element.8.rolled_at, s32[32,128]{1,0:T(8,128)} %get-tuple-element.7.slot_at, s32[32,128]{1,0:T(8,128)} %get-tuple-element.6.onsite_at, s32[32,128]{1,0:T(8,128)} %get-tuple-element.5.part_at, f32[32,128]{1,0:T(8,128)} %fusion.active, ...), custom_call_target="tpu_custom_call" | custom-call | tf_op jit(solution)/shard_map/density/pallas_call | solution.py:362
  111.0 1.7 %copy.8 = f32[128,3,2048]{2,0,1:T(8,128)} copy(f32[128,3,2048]{2,0,1:T(8,128)S(1)} %bitcast.11) | data formatting | bytes 6291456
  (1 shorter events, 0.0 us)

commit v3 on v2

--- a/solution.py
+++ b/solution.py
@@ -101,7 +101,7 @@
 
 
 def kernel(
-    listed, rolled_at, slot_at, onsite_at, part_at, active, inverse, ham_in, pattern, onsite, inv_in, out,
+    listed, rolled_at, slot_at, onsite_at, part_at, orders, inverse, ham_in, pattern, onsite, inv_in, out,
     ham, inv_tiles, own, onsites, left, rolled, turned, mat, diag, placed, local_sems, sems, *scratch
 ):
     row, col, y, z, device = places()
@@ -120,6 +120,12 @@
     bufs, signs = scratch[:SLOTS], scratch[SLOTS:]
     for ref in signs:
         ref[0] = jnp.zeros((BLOCK, OWN), BF16)
+    for ref in bufs:
+        ref[TEAM_BLOCKS] = jnp.zeros((BLOCK, OWN), BF16)
+    own[TEAM_BLOCKS] = jnp.zeros((BLOCK, OWN), F32)
+    onsites[4 * SLOTS] = jnp.zeros((1, OWN), F32)
+    rolled[4 * SLOTS] = jnp.zeros((TILES, OWN, OWN), BF16)
+    turned[SLOTS] = jnp.zeros((TILES, OWN_BLOCKS, BLOCK, OWN), BF16)
     lanes = lax.broadcasted_iota(jnp.int32, (OWN_BLOCKS, OWN), 1) // BLOCK
     spread = (lanes == lax.broadcasted_iota(jnp.int32, (OWN_BLOCKS, OWN), 0)).astype(F32)
     weights = lax.dot_general(
@@ -142,8 +148,7 @@
     one_row = lax.broadcasted_iota(jnp.int32, (1, OWN), 1) // BLOCK
 
     def blocks(read, tile):
-        pieces = [read(listed[tile * 4 + q, group]).astype(F32) * active[tile * 4 + q, group] for q in range(4)]
-        return jnp.concatenate(pieces, axis=0)
+        return jnp.concatenate([read(listed[tile * 4 + q, group]) for q in range(4)], axis=0)
 
     @pl.loop(0, TILES)
     def _(tile):
@@ -151,7 +156,7 @@
         left[:, at] = blocks(lambda m: own[m], tile).T
         picked = jnp.zeros((1, OWN), F32)
         for q in range(4):
-            line = onsites[onsite_at[tile * 4 + q, group]] * active[tile * 4 + q, group]
+            line = onsites[onsite_at[tile * 4 + q, group]]
             picked = jnp.where(one_row == q, line, picked)
         diag[:, at] = picked
 
@@ -161,8 +166,9 @@
         @pl.loop(0, TILES)
         def _(tile):
             x = blocks(lambda m: bufs[slot][m], tile)
+            rolled[slot * 4, tile] = x
+            x = x.astype(F32)
             turned[slot, tile] = x.T.astype(BF16).reshape(4, BLOCK, OWN)
-            rolled[slot * 4, tile] = x.astype(BF16)
             for s in (1, 2, 3):
                 rolled[slot * 4 + s, tile] = pltpu.roll(x, s * BLOCK, axis=1).astype(BF16)
 
@@ -178,7 +184,7 @@
     def direct(up, over):
         tile = None
         for q in range(4):
-            piece = rolled[rolled_at[over * 4 + q, group], up].astype(F32) * active[over * 4 + q, group]
+            piece = rolled[rolled_at[over * 4 + q, group], up].astype(F32)
             tile = piece if tile is None else jnp.where(which == q, piece, tile)
         return tile
 
@@ -186,8 +192,8 @@
         pieces = []
         for q in range(4):
             a = up * 4 + q
-            pieces.append(turned[slot_at[a, group], over, part_at[a, group]].astype(F32) * active[a, group])
-        return jnp.concatenate(pieces, axis=0)
+            pieces.append(turned[slot_at[a, group], over, part_at[a, group]])
+        return jnp.concatenate(pieces, axis=0).astype(F32)
 
     def assemble(n, total):
         up, over = n // TILES, n % TILES
@@ -210,24 +216,26 @@
         if tile == 0:
             first += jnp.where(eye, energy, 0.0)
         start.append(first)
-    count = 0.0
-    for a in range(MEMBERS):
-        count += active[a, group] * float(BLOCK)
+    count = (orders[group] * BLOCK).astype(F32)
     squares = jnp.sum(jnp.sum(total, axis=0, keepdims=True) + extra, axis=1, keepdims=True)
     scale = jnp.sqrt(count / (4.0 * (squares + 1e-06)))
     energy = diag[...]
 
-    def apply(x):
+    def apply(x, split=False):
         high = x.astype(BF16)
-        low = (x - high.astype(F32)).astype(BF16)
-        y = jnp.dot(jnp.concatenate([high, low], axis=0), mat[...], preferred_element_type=F32)
-        return scale * (y[:OWN] + y[OWN:] + x * energy)
+        if split:
+            low = (x - high.astype(F32)).astype(BF16)
+            y = jnp.dot(jnp.concatenate([high, low], axis=0), mat[...], preferred_element_type=F32)
+            y = y[:OWN] + y[OWN:]
+        else:
+            y = jnp.dot(high, mat[...], preferred_element_type=F32)
+        return scale * (y + x * energy)
 
     initial = scale * jnp.concatenate(start, axis=1)
     first_step = 1.5 * initial - 0.5 * apply(apply(initial))
-    once = apply(first_step)
+    once = apply(first_step, split=True)
     once = 1.5 * once - 0.5 * apply(apply(once))
-    twice = apply(once)
+    twice = apply(once, split=True)
     twice = 1.5 * twice - 0.5 * apply(apply(twice))
     result = 1.5 * first_step - 0.5 * twice
     for tile in range(TILES):
@@ -358,7 +366,17 @@
     part, block = listed & 3, listed >> 2
     slot = (((block >> 2) - (col >> 2)) & 3) * 4 + ((block - col) & 3)
     turn = (at - part) & 3
-    active = (at < orders).astype(F32)
+    active = at < orders
+    tables = [
+        jnp.where(active, values, idle)
+        for values, idle in (
+            (listed, TEAM_BLOCKS),
+            (slot * 4 + turn, SLOTS * 4),
+            (slot, SLOTS),
+            (turn * SLOTS + block, SLOTS * 4),
+            (part, 0),
+        )
+    ]
     density = pl.pallas_call(
         kernel,
         out_shape=pltpu.VMEM((3, OWN, TEAM_WIDTH), F32),
@@ -367,17 +385,17 @@
         scratch_shapes=[
             pltpu.VMEM((TEAM_WIDTH, OWN), F32),
             pltpu.VMEM((3, OWN, TEAM_WIDTH), BF16),
-            pltpu.VMEM((TEAM_BLOCKS, BLOCK, OWN), F32),
-            pltpu.VMEM((4 * SLOTS, 1, OWN), F32),
+            pltpu.VMEM((TEAM_BLOCKS + 1, BLOCK, OWN), F32),
+            pltpu.VMEM((4 * SLOTS + 1, 1, OWN), F32),
             pltpu.VMEM((OWN, SUB), F32),
-            pltpu.VMEM((SLOTS * 4, TILES, OWN, OWN), BF16),
-            pltpu.VMEM((SLOTS, TILES, OWN_BLOCKS, BLOCK, OWN), BF16),
+            pltpu.VMEM((SLOTS * 4 + 1, TILES, OWN, OWN), BF16),
+            pltpu.VMEM((SLOTS + 1, TILES, OWN_BLOCKS, BLOCK, OWN), BF16),
             pltpu.VMEM((SUB, SUB), BF16),
             pltpu.VMEM((1, SUB), F32),
             pltpu.VMEM((TEAM_WIDTH, 2 * OWN), BF16),
             pltpu.SemaphoreType.DMA((2,)),
             pltpu.SemaphoreType.DMA((2, 170)),
-            *[pltpu.VMEM((TEAM_BLOCKS, BLOCK, OWN), BF16) for _ in range(SLOTS)],
+            *[pltpu.VMEM((TEAM_BLOCKS + 1, BLOCK, OWN), BF16) for _ in range(SLOTS)],
             *[pltpu.VMEM((MEMBERS + 1, BLOCK, OWN), BF16) for _ in range(3 * SLOTS)],
         ],
         compiler_params=pltpu.CompilerParams(
@@ -385,12 +403,8 @@
         ),
         name="density",
     )(
-        listed,
-        slot * 4 + turn,
-        slot,
-        turn * SLOTS + block,
-        part,
-        active,
+        *tables,
+        orders,
         inverse,
         hamiltonian,
         pattern.T,

time: 113 us -> 109 us (0.965)
  Pallas kernels: 107 us -> 104 us
  other arithmetic: 4.12 us -> 2.89 us
    pallas_call x1, Pallas kernels: 107 us -> 104 us  [shards(): pl.pallas_call(kernel, out_shape=pltpu.VMEM((3, OWN, TEAM_WIDTH), F32), i...]
    select_n x0 -> x1, other arithmetic: none -> 1.37 us  [shards(): jnp.where(active, values, idle)]
    and x1 -> x0, other arithmetic: 1.35 us -> none  [shards(): part, block = (listed & 3, listed >> 2)]
    convert_element_type x1 -> x0, other arithmetic: 1.26 us -> none  [shards(): active = (at < orders).astype(F32)]
where the time goes in v3:
time: 109 us
  Pallas kernels  104 us (95%)
  other arithmetic  2.89 us (3%)
  local copies, waits for them, and re-layouts  1.67 us (2%)
    pallas_call x1, Pallas kernels, shards(): pl.pallas_call(kernel, out_shape=pltpu.VMEM((3, OWN, TEAM_WIDTH), F32), i...  104 us

profile of v3, /device:TPU:1, one launch (start us, length us, event | category | flops | bytes accessed | tf_op | source)
XLA Modules:
  0.0 109.0 jit_solution(16622351631892758948)
XLA Ops:
  0.0 1.5 %select_reduce_fusion.inverse = s32[64,128]{1,0:T(8,128)} fusion(s32[32]{0:T(128)S(1)} %iota_add_fusion, s32[32,128]{1,0:T(8,128)} %bitcast.12), kind=kLoop, calls=%fused_computation | loop fusion | flops 778240 | bytes 49280 | tf_op jit(solution)/shard_map/reduce_sum | solution.py:363
  1.5 1.4 %fusion = (s32[32,128]{1,0:T(8,128)}, s32[32,128]{1,0:T(8,128)}, s32[32,128]{1,0:T(8,128)}, s32[32,128]{1,0:T(8,128)}, s32[32,128]{1,0:T(8,128)}) fusion(s32[128]{0:T(128)} %orders.1, s32[128,32]{0,1:T(8,128)} %param.9, s32[]{:T(128)S(6)} %axis_index.12, s32[]{:T(128)S(6)} %shift_right_arithmetic.11), kind=kLoop, calls=%fused_computation.7 | loop fusion | flops 86016 | bytes 98824 | tf_op jit(solution)/shard_map/jit(_where)/select_n | solution.py:371
  2.9 104.4 %density.1 = f32[3,128,2048]{2,1,0:T(8,128)S(1)} custom-call(s32[32,128]{1,0:T(8,128)} %get-tuple-element.9.listed, s32[32,128]{1,0:T(8,128)} %get-tuple-element.8.rolled_at, s32[32,128]{1,0:T(8,128)} %get-tuple-element.7.slot_at, s32[32,128]{1,0:T(8,128)} %get-tuple-element.6.onsite_at, s32[32,128]{1,0:T(8,128)} %get-tuple-element.5.part_at, s32[128]{0:T(128)} %orders.1, ...), custom_call_target="tpu_custom_call" | custom-call | tf_op jit(solution)/shard_map/density/pallas_call | solution.py:380
  107.3 1.7 %copy.8 = f32[128,3,2048]{2,0,1:T(8,128)} copy(f32[128,3,2048]{2,0,1:T(8,128)S(1)} %bitcast.10) | data formatting | bytes 6291456
  (1 shorter events, 0.0 us)

commit v4 on v3

--- a/solution.py
+++ b/solution.py
@@ -203,7 +203,7 @@
         )
         return total + jnp.sum((tile * tile).reshape(OWN // 8, 8, OWN), axis=0)
 
-    total = lax.fori_loop(0, TILES * TILES, assemble, jnp.zeros((8, OWN), F32))
+    total = lax.fori_loop(0, TILES * TILES, assemble, jnp.zeros((8, OWN), F32), unroll=4)
 
     extra = jnp.zeros((1, OWN), F32)
     start = []

time: 109 us -> 109 us (level)
  no operation moved by 1% of the time
where the time goes in v4:
time: 109 us
  Pallas kernels  104 us (95%)
  other arithmetic  2.89 us (3%)
  local copies, waits for them, and re-layouts  1.67 us (2%)
    pallas_call x1, Pallas kernels, shards(): pl.pallas_call(kernel, out_shape=pltpu.VMEM((3, OWN, TEAM_WIDTH), F32), i...  104 us

profile of v4, /device:TPU:1, one launch (start us, length us, event | category | flops | bytes accessed | tf_op | source)
XLA Modules:
  0.0 108.5 jit_solution(13347202724989259654)
XLA Ops:
  0.0 1.5 %select_reduce_fusion.inverse = s32[64,128]{1,0:T(8,128)} fusion(s32[32]{0:T(128)S(1)} %iota_add_fusion, s32[32,128]{1,0:T(8,128)} %bitcast.12), kind=kLoop, calls=%fused_computation | loop fusion | flops 778240 | bytes 49280 | tf_op jit(solution)/shard_map/reduce_sum | solution.py:363
  1.5 1.4 %fusion = (s32[32,128]{1,0:T(8,128)}, s32[32,128]{1,0:T(8,128)}, s32[32,128]{1,0:T(8,128)}, s32[32,128]{1,0:T(8,128)}, s32[32,128]{1,0:T(8,128)}) fusion(s32[128]{0:T(128)} %orders.1, s32[128,32]{0,1:T(8,128)} %param.9, s32[]{:T(128)S(6)} %axis_index.12, s32[]{:T(128)S(6)} %shift_right_arithmetic.11), kind=kLoop, calls=%fused_computation.7 | loop fusion | flops 86016 | bytes 98824 | tf_op jit(solution)/shard_map/jit(_where)/select_n | solution.py:371
  2.9 104.0 %density.1 = f32[3,128,2048]{2,1,0:T(8,128)S(1)} custom-call(s32[32,128]{1,0:T(8,128)} %get-tuple-element.9.listed, s32[32,128]{1,0:T(8,128)} %get-tuple-element.8.rolled_at, s32[32,128]{1,0:T(8,128)} %get-tuple-element.7.slot_at, s32[32,128]{1,0:T(8,128)} %get-tuple-element.6.onsite_at, s32[32,128]{1,0:T(8,128)} %get-tuple-element.5.part_at, s32[128]{0:T(128)} %orders.1, ...), custom_call_target="tpu_custom_call" | custom-call | tf_op jit(solution)/shard_map/density/pallas_call | solution.py:380
  106.9 1.7 %copy.8 = f32[128,3,2048]{2,0,1:T(8,128)} copy(f32[128,3,2048]{2,0,1:T(8,128)S(1)} %bitcast.10) | data formatting | bytes 6291456
  (1 shorter events, 0.0 us)
